TPU v7x, 32 devices: a whole 2x2x4 slice. The times are simulated.
32 devices in a mesh: parts: 2 (over x), wide: 16 (over z, y, core).
Axes of the slice: x: 2, y: 2, z: 4, core: 2. Of those that a mesh axis runs over, the one named last changes fastest.
Arguments:
- tokens: bfloat16 [384, 7168], P(('parts', 'wide')), parts along dimension 0, may hold values from -6 to 6
- expert_ids: int32 [384, 8], P(('parts', 'wide')), parts along dimension 0, may hold values from 0 to 15, as said below
- gates: float32 [384, 8], P(('parts', 'wide')), parts along dimension 0, may hold values from 0.1 to 1
- w_gate: bfloat16 [2, 7168, 8192], P(None, None, 'wide'), may hold values from -0.0625 to 0.0625
- w_up: bfloat16 [2, 7168, 8192], P(None, None, 'wide'), may hold values from -0.0625 to 0.0625
- w_down: bfloat16 [2, 8192, 7168], P(None, 'wide'), may hold values from -0.1875 to 0.1875
Outputs:
- moe_out: bfloat16 [384, 7168], P(('parts', 'wide')), parts along dimension 0
There are 2 independent parts, one for each index of `parts`. A program takes and returns all parts, laid end to end along the dimension named above; an argument that names none is the same for every part. Nothing has to cross between parts.
Inputs may be any that keep to these rules, and one draw needn't show every extreme that they name: `expert_ids`: each row names the 2 experts g * 2 to g * 2 + 1 of each of 4 different groups g, in any order; in each part one group is named by every row.
All inputs are finite; a program needn't handle non-finite values.
Results may differ from a plain program's by a relative error of at most 0.0064.
Values may be sent and summed in bfloat16 or wider, within the bound.
A program may use at most 128 MiB of HBM per device.

v0:
```python
import jax
import jax.numpy as jnp
from jax import lax
from jax.sharding import PartitionSpec as P

GROUPS = 8
EXP_G = 2


def partner(block, axis, bit):
    count = lax.axis_size(axis)
    route = []
    for low in range(count):
        high = low | 1 << bit
        if high != low and high < count:
            route += [(low, high), (high, low)]
    return lax.ppermute(block, axis, route)


def route_table(expert_ids, gates):
    token_count = expert_ids.shape[0]
    catalog = jnp.arange(GROUPS * EXP_G, dtype=jnp.int32)
    picked = expert_ids[:, :, None] == catalog[None, None, :]
    weight_sum = jnp.sum(jnp.where(picked, gates[:, :, None], 0.0), axis=1)
    return weight_sum.astype(jnp.bfloat16).reshape(token_count, GROUPS, EXP_G)


def selection(expert_ids, wide_count, group_size, slot_count):
    token_count = expert_ids.shape[0]
    group_ids = jnp.arange(GROUPS, dtype=jnp.int32)
    member = jnp.any((expert_ids // EXP_G)[:, :, None] == group_ids[None, None, :], axis=1)
    position = jnp.cumsum(member.astype(jnp.int32), axis=0) - 1
    target = jnp.arange(wide_count, dtype=jnp.int32)
    target_group = (target // group_size)[:, None] == group_ids[None, :]
    target_rank = target % group_size
    member_dest = jnp.any(target_group[:, :, None] & member.T[None, :, :], axis=1)
    position_dest = jnp.sum(jnp.where(target_group[:, :, None], position.T[None, :, :], 0), axis=1)
    stride = token_count // slot_count
    wanted = (
        jnp.arange(slot_count, dtype=jnp.int32)[None, :] * stride + (target_rank % stride)[:, None]
    )
    chosen = member_dest[:, None, :] & (position_dest[:, None, :] == wanted[:, :, None])
    return (chosen, target_group)


def pack(tokens, route_weight, chosen, target_group):
    wide_count, slot_count, token_count = chosen.shape
    pick_table = chosen.astype(jnp.bfloat16).reshape(wide_count * slot_count, token_count)
    packed = jnp.dot(pick_table, tokens, preferred_element_type=jnp.float32).astype(jnp.bfloat16)
    packed = packed.reshape(wide_count, slot_count, tokens.shape[1])
    route_dest = jnp.einsum(
        "dg,tgj->dtj",
        target_group.astype(jnp.float32),
        route_weight.astype(jnp.float32),
        precision=lax.Precision.HIGHEST,
    )
    scaled = jnp.einsum(
        "dst,dtj->dsj", chosen.astype(jnp.float32), route_dest, precision=lax.Precision.HIGHEST
    )
    return (packed, scaled.astype(jnp.bfloat16))


def expert_block(inputs, scales, w_gate, w_up, w_down):
    summed = jnp.zeros((inputs.shape[0], w_down.shape[2]), jnp.float32)
    for expert in range(EXP_G):
        gate_value = jnp.dot(inputs, w_gate[expert], preferred_element_type=jnp.float32)
        lifted = jnp.dot(inputs, w_up[expert], preferred_element_type=jnp.float32)
        hidden = (jax.nn.silu(gate_value) * lifted).astype(jnp.bfloat16)
        summed = summed + scales[:, expert : expert + 1].astype(jnp.float32) * jnp.dot(
            hidden, w_down[expert], preferred_element_type=jnp.float32
        )
    return summed.astype(jnp.bfloat16)


def local(tokens, expert_ids, gates, w_gate, w_up, w_down):
    wide_count = lax.axis_size("wide")
    group_size = wide_count // GROUPS
    token_count = tokens.shape[0]
    model_width = tokens.shape[1]
    route_weight = route_table(expert_ids, gates)
    slot_count = token_count // group_size
    chosen, target_group = selection(expert_ids, wide_count, group_size, slot_count)
    packed, scaled = pack(tokens, route_weight, chosen, target_group)
    arrived, arrived_scale = (
        lax.all_to_all(packed, "wide", split_axis=0, concat_axis=0, tiled=True),
        lax.all_to_all(scaled, "wide", split_axis=0, concat_axis=0, tiled=True),
    )
    my_rank = lax.axis_index("wide") % group_size
    levels = group_size.bit_length() - 1
    held_rows = arrived[None]
    held_scale = arrived_scale[None]
    for level_index in range(levels):
        partner_rows, partner_scale = partner((held_rows, held_scale), "wide", level_index)
        upper_half = my_rank // (1 << level_index) % 2 == 1
        held_rows = jnp.concatenate(
            [
                jnp.where(upper_half, partner_rows, held_rows),
                jnp.where(upper_half, held_rows, partner_rows),
            ],
            0,
        )
        held_scale = jnp.concatenate(
            [
                jnp.where(upper_half, partner_scale, held_scale),
                jnp.where(upper_half, held_scale, partner_scale),
            ],
            0,
        )
    partial_value = expert_block(
        held_rows.reshape(-1, model_width), held_scale.reshape(-1, EXP_G), w_gate, w_up, w_down
    )
    partial_value = partial_value.reshape(group_size, wide_count, slot_count, model_width)
    returned = lax.all_to_all(partial_value, "wide", split_axis=1, concat_axis=1, tiled=True)
    chosen_grouped = chosen.reshape(GROUPS, group_size, slot_count, token_count).transpose(
        1, 0, 2, 3
    )
    pick_rows = jnp.broadcast_to(
        chosen_grouped[:, :, None], (group_size, GROUPS, group_size, slot_count, token_count)
    )
    pick_table = pick_rows.reshape(group_size * wide_count * slot_count, token_count).T.astype(
        jnp.bfloat16
    )
    output = jnp.dot(
        pick_table, returned.reshape(-1, model_width), preferred_element_type=jnp.float32
    )
    return output.astype(jnp.bfloat16)


def solution(mesh):
    return jax.shard_map(
        local,
        mesh=mesh,
        in_specs=(
            P(("parts", "wide"), None),
            P(("parts", "wide"), None),
            P(("parts", "wide"), None),
            P(None, None, "wide"),
            P(None, None, "wide"),
            P(None, "wide", None),
        ),
        out_specs=P(("parts", "wide"), None),
        check_vma=False,
    )
```

profile of v0, /device:TPU:15, one launch (start us, length us, event | category | flops | bytes accessed | tf_op | source)
XLA Modules:
  0.0 191.6 jit_solution(12496329950907122249)
XLA Ops:
  0.0 0.8 add_select_fusion
  2.7 1.5 reshape.140
  4.2 6.5 %all-to-all-start.1 = ((bf16[16,6,7168]{2,1,0:T(8,128)(2,1)}), bf16[16,6,7168]{2,1,0:T(8,128)(2,1)S(1)}, u32[]{:S(2)}, u32[]{:S(2)}) async-start(bf16[16,6,7168]{2,1,0:T(8,128)(2,1)} %reshape.140), calls=%async_computation.1 | async-start | bytes 3670016 | tf_op jit(solution)/shard_map/all_to_all | solution.py:85
  11.1 41.4 %all-to-all-done.1 = bf16[16,6,7168]{2,1,0:T(8,128)(2,1)S(1)} async-done(((bf16[16,6,7168]{2,1,0:T(8,128)(2,1)}), bf16[16,6,7168]{2,1,0:T(8,128)(2,1)S(1)}, u32[]{:S(2)}, u32[]{:S(2)}) %all-to-all-start.1) | async-done | bytes 1376288 | tf_op jit(solution)/shard_map/all_to_all | solution.py:85
  52.5 1.9 copy.64
  54.9 0.8 convolution_convert_fusion.2
  55.7 5.1 %all-to-all-start = ((bf16[16,6,2]{1,2,0:T(2,128)(2,1)}), bf16[16,6,2]{1,2,0:T(2,128)(2,1)S(1)}, u32[]{:S(2)}, u32[]{:S(2)}) async-start(bf16[16,6,2]{1,2,0:T(2,128)(2,1)} %convolution_convert_fusion.2), calls=%async_computation | async-start | bytes 16384 | tf_op jit(solution)/shard_map/all_to_all | solution.py:86
  60.7 3.8 %all-to-all-done = bf16[16,6,2]{1,2,0:T(2,128)(2,1)S(1)} async-done(((bf16[16,6,2]{1,2,0:T(2,128)(2,1)}), bf16[16,6,2]{1,2,0:T(2,128)(2,1)S(1)}, u32[]{:S(2)}, u32[]{:S(2)}) %all-to-all-start) | async-done | bytes 416 | tf_op jit(solution)/shard_map/all_to_all | solution.py:86
  64.5 0.7 collective-permute-start
  65.2 0.8 collective-permute-done
  66.2 1.7 copy_select_fusion.1
  67.9 2.6 %pad_maximum_fusion = bf16[2,16,6,7168]{3,2,1,0:T(8,128)(2,1)} fusion(bf16[1,16,6,7168]{3,2,1,0:T(8,128)(2,1)S(1)} %get-tuple-element.6, bf16[1,16,6,7168]{3,2,1,0:T(8,128)(2,1)S(1)} %get-tuple-element.5), kind=kLoop, calls=%fused_computation.22 | loop fusion | flops 1376256 | bytes 5505024 | tf_op jit(solution)/shard_map/concatenate | solution.py:95
  70.5 3.2 %reshape.141 = bf16[192,7168]{1,0:T(8,128)(2,1)S(1)} reshape(bf16[2,16,6,7168]{3,2,1,0:T(8,128)(2,1)} %pad_maximum_fusion) | data formatting | bytes 5505024 | tf_op jit(solution)/shard_map/reshape | solution.py:110
  73.7 5.5 %fusion.3 = f32[192,512]{1,0:T(8,128)} fusion(bf16[192,7168]{1,0:T(8,128)(2,1)S(1)} %reshape.141, bf16[2,7168,512]{2,1,0:T(8,128)(2,1)} %param.10), kind=kOutput, calls=%fused_computation.7 | convolution fusion | flops 1409286144 | bytes 10485760 | tf_op jit(solution)/shard_map/dot_general | solution.py:67
  79.2 4.7 %fusion.8 = f32[192,512]{1,0:T(8,128)S(1)} fusion(bf16[192,7168]{1,0:T(8,128)(2,1)S(1)} %reshape.141, bf16[2,7168,512]{2,1,0:T(8,128)(2,1)} %param.10), kind=kOutput, calls=%fused_computation.12 | convolution fusion | flops 1409286144 | bytes 10485760 | tf_op jit(solution)/shard_map/dot_general | solution.py:67
  83.9 10.9 %convolution_multiply_fusion = f32[192,7168]{1,0:T(8,128)} fusion(bf16[2,512,7168]{2,1,0:T(8,128)(2,1)} %param.11, f32[192]{0:T(256)S(1)} %bitcast.69, f32[192,512]{1,0:T(8,128)} %fusion.3, bf16[192,7168]{1,0:T(8,128)(2,1)S(1)} %reshape.141, bf16[2,7168,512]{2,1,0:T(8,128)(2,1)} %param.9), kind=kOutput, calls=%fused_computation | convolution fusion | flops 2820538368 | bytes 23331584 | tf_op jit(solution)/shard_map/dot_general | solution.py:69
  94.8 11.4 %fusion.1 = bf16[192,7168]{1,0:T(8,128)(2,1)} fusion(f32[192,7168]{1,0:T(8,128)} %convolution_multiply_fusion, bf16[2,512,7168]{2,1,0:T(8,128)(2,1)} %param.11, f32[192]{0:T(256)S(1)} %bitcast.68, f32[192,512]{1,0:T(8,128)S(1)} %fusion.8, bf16[192,7168]{1,0:T(8,128)(2,1)S(1)} %reshape.141, bf16[2,7168,512]{2,1,0:T(8,128)(2,1)} %param.9), kind=kOutput, calls=%fused_computation.3 | convolution fusion | flops 2823290880 | bytes 26084096 | tf_op jit(solution)/shard_map/dot_general | solution.py:69
  106.2 4.6 %reshape.142 = bf16[2,16,6,7168]{3,2,1,0:T(8,128)(2,1)} reshape(bf16[192,7168]{1,0:T(8,128)(2,1)} %fusion.1) | data formatting | bytes 5505024 | tf_op jit(solution)/shard_map/reshape | solution.py:112
  110.8 6.4 %copy.67 = bf16[2,16,6,7168]{3,0,2,1:T(2,128)(2,1)} copy(bf16[2,16,6,7168]{3,2,1,0:T(8,128)(2,1)} %reshape.142) | data formatting | bytes 5505024 | tf_op jit(solution)/shard_map/reshape | solution.py:112
  117.2 5.9 %all-to-all-start.2 = ((bf16[2,16,6,7168]{3,0,2,1:T(2,128)(2,1)}), bf16[2,16,6,7168]{3,0,2,1:T(2,128)(2,1)S(1)}, u32[]{:S(2)}, u32[]{:S(2)}) async-start(bf16[2,16,6,7168]{3,0,2,1:T(2,128)(2,1)} %copy.67), calls=%async_computation.2 | async-start | bytes 5505024 | tf_op jit(solution)/shard_map/all_to_all | solution.py:113
  123.6 61.0 %all-to-all-done.2 = bf16[2,16,6,7168]{3,0,2,1:T(2,128)(2,1)S(1)} async-done(((bf16[2,16,6,7168]{3,0,2,1:T(2,128)(2,1)}), bf16[2,16,6,7168]{3,0,2,1:T(2,128)(2,1)S(1)}, u32[]{:S(2)}, u32[]{:S(2)}) %all-to-all-start.2) | async-done | bytes 2752544 | tf_op jit(solution)/shard_map/all_to_all | solution.py:113
  184.6 2.5 %copy.68 = bf16[2,16,6,7168]{3,2,1,0:T(8,128)(2,1)} copy(bf16[2,16,6,7168]{3,0,2,1:T(2,128)(2,1)S(1)} %all-to-all-done.2) | data formatting | bytes 5505024 | tf_op jit(solution)/shard_map/all_to_all | solution.py:113
  187.2 3.2 %reshape.143 = bf16[192,7168]{1,0:T(8,128)(2,1)S(1)} reshape(bf16[2,16,6,7168]{3,2,1,0:T(8,128)(2,1)} %copy.68) | data formatting | bytes 5505024 | tf_op jit(solution)/shard_map/reshape | solution.py:124
  190.4 1.2 convolution_convert_fusion.1
  (54 shorter events, 3.3 us)
Async XLA Ops:
  0.0 2.1 %copy-start = (bf16[12,7168]{1,0:T(8,128)(2,1)S(1)}, bf16[12,7168]{1,0:T(8,128)(2,1)}, u32[]{:S(2)}) copy-start(bf16[12,7168]{1,0:T(8,128)(2,1)} %param.6) | copy-start | bytes 516100
  2.6 8.1 %copy-start.2 = (s32[12,8]{0,1:T(8,128)S(1)}, s32[12,8]{0,1:T(8,128)}, u32[]{:S(2)}) copy-start(s32[12,8]{0,1:T(8,128)} %param.7) | copy-start | bytes 1156
  2.7 8.2 %copy-start.3 = (f32[12,8]{0,1:T(8,128)S(1)}, f32[12,8]{0,1:T(8,128)}, u32[]{:S(2)}) copy-start(f32[12,8]{0,1:T(8,128)} %param.8) | copy-start | bytes 1156
  4.2 48.3 %all-to-all-start.1 = ((bf16[16,6,7168]{2,1,0:T(8,128)(2,1)}), bf16[16,6,7168]{2,1,0:T(8,128)(2,1)S(1)}, u32[]{:S(2)}, u32[]{:S(2)}) async-start(bf16[16,6,7168]{2,1,0:T(8,128)(2,1)} %reshape.140), calls=%async_computation.1 | async-start | bytes 3670016 | tf_op jit(solution)/shard_map/all_to_all | solution.py:85
  54.4 11.8 %collective-permute-start.1 = (bf16[1,16,6,7168]{3,1,2,0:T(8,128)(2,1)}, bf16[1,16,6,7168]{3,1,2,0:T(8,128)(2,1)S(1)}, u32[]{:S(2)}, u32[]{:S(2)}) collective-permute-start(bf16[1,16,6,7168]{3,1,2,0:T(8,128)(2,1)} %copy.64), channel_id=1, source_target_pairs={{0,1},{1,0},{2,3},{3,2},{4,5},{5,4},{6,7},{7,6},{8,9},{9,8},{10,11... | collective-permute-start | bytes 4128776 | tf_op jit(solution)/shard_map/ppermute | solution.py:17
  55.7 8.9 %all-to-all-start = ((bf16[16,6,2]{1,2,0:T(2,128)(2,1)}), bf16[16,6,2]{1,2,0:T(2,128)(2,1)S(1)}, u32[]{:S(2)}, u32[]{:S(2)}) async-start(bf16[16,6,2]{1,2,0:T(2,128)(2,1)} %convolution_convert_fusion.2), calls=%async_computation | async-start | bytes 16384 | tf_op jit(solution)/shard_map/all_to_all | solution.py:86
  64.5 1.5 collective-permute-start
  117.2 67.4 %all-to-all-start.2 = ((bf16[2,16,6,7168]{3,0,2,1:T(2,128)(2,1)}), bf16[2,16,6,7168]{3,0,2,1:T(2,128)(2,1)S(1)}, u32[]{:S(2)}, u32[]{:S(2)}) async-start(bf16[2,16,6,7168]{3,0,2,1:T(2,128)(2,1)} %copy.67), calls=%async_computation.2 | async-start | bytes 5505024 | tf_op jit(solution)/shard_map/all_to_all | solution.py:113
  184.6 7.0 %copy-start.1 = (bf16[12,7168]{1,0:T(8,128)(2,1)S(1)}, bf16[12,7168]{1,0:T(8,128)(2,1)}, u32[]{:S(2)}) copy-start(bf16[12,7168]{1,0:T(8,128)(2,1)} %param.6) | copy-start | bytes 516100
where the time goes:
time: 192 us
  waiting for transfers between devices  107 us (56%)
  matrix products  35.2 us (18%)
  local copies, waits for them, and re-layouts  24.9 us (13%)
  starting transfers between devices  18.3 us (10%)
  other arithmetic  5.96 us (3%)
    all_to_all x1, waiting for transfers between devices, local(): lax.all_to_all(partial_value, 'wide', split_axis=1, concat_axis=1, tiled=...  61 us
    all_to_all x1, waiting for transfers between devices, local(): lax.all_to_all(packed, 'wide', split_axis=0, concat_axis=0, tiled=True)  41.4 us
    dot_general x2, matrix products, expert_block(): jnp.dot(hidden, w_down[expert], preferred_element_type=jnp.float32)  22.3 us
    reshape x2, local copies, waits for them, and re-layouts, local(): partial_value.reshape(group_size, wide_count, slot_count, model_width)  11 us
    dot_general x2, matrix products, expert_block(): lifted = jnp.dot(inputs, w_up[expert], preferred_element_type=jnp.float32)  10.1 us
    all_to_all x1, starting transfers between devices, local(): lax.all_to_all(packed, 'wide', split_axis=0, concat_axis=0, tiled=True)  6.52 us
    all_to_all x1, starting transfers between devices, local(): lax.all_to_all(partial_value, 'wide', split_axis=1, concat_axis=1, tiled=...  5.92 us
    all_to_all x1, starting transfers between devices, local(): lax.all_to_all(scaled, 'wide', split_axis=0, concat_axis=0, tiled=True)  5.06 us
  transfers between devices with their start and end apart: 5, of which 4 were waited for; matrix products, arithmetic and copies ran while one was open for 1% of the time, Pallas kernels for 0%

commit v1 on v0

v1 whole, which is shorter than its diff:
```python
import functools
import math

import jax
import jax.numpy as jnp
from jax import lax
from jax.experimental import pallas as pl
from jax.experimental.pallas import tpu as pltpu
from jax.sharding import PartitionSpec as P

GROUPS = 8
EXP_G = 2
CORES = 2
SIDES = 2
CHUNK = 256
LANES = 128
F32 = jnp.float32
BF16 = jnp.bfloat16


def floor_div(value, by):
    return jnp.floor((value + 0.5) * (1.0 / by))


def iota_f32(shape, dim):
    return lax.broadcasted_iota(jnp.int32, shape, dim).astype(F32)


def kernel(
    wide, rows, fold,
    x_ref, r_ref, wg_ref, wu_ref, wd_ref, out_ref,
    xb, rb, wgb, wub, wdb, acc, hid, perm, perm_back, packed, got_core, sum_side, got_side, sum_z, got_z, out_buf,
    w_sem, d_sem, own_sem, az_s, az_r, ay_s, ay_r, ac_s, ac_r, bz_s, bz_r, by_s, by_r, bc_s, bc_r, out_sem,
):
    zs = wide // (CORES * SIDES)
    chunks = x_ref.shape[0]
    hidden = wg_ref.shape[2]
    width = chunks * CHUNK
    unit = rows * fold
    units = wide
    groups = units // fold
    band = fold * rows
    pad_rows = r_ref.shape[0]

    me = lax.axis_index("wide")
    core = lax.rem(me, CORES)
    chip = me // CORES
    side = lax.rem(chip, SIDES)
    z = chip // SIDES
    other_core = 1 - core
    other_side = 1 - side

    def at(z_at, side_at, core_at):
        return {"wide": (z_at * SIDES + side_at) * CORES + core_at}

    core_dev = at(z, side, other_core)
    side_dev = at(z, other_side, core)

    def z_of(step):
        return lax.rem(z + step, zs)

    def send(src, dst, s_sem, r_sem, dev):
        return pltpu.make_async_remote_copy(
            src_ref=src, dst_ref=dst, send_sem=s_sem, recv_sem=r_sem, device_id=dev, device_id_type=pl.DeviceIdType.MESH
        )

    def up_copies(k):
        copies = []
        for block in range(fold):
            source = pl.ds(pl.multiple_of(block * width + k * CHUNK, CHUNK), CHUNK)
            target = pl.ds(block * CHUNK, CHUNK)
            for expert in range(EXP_G):
                copies.append(pltpu.make_async_copy(wg_ref.at[expert, source, :], wgb.at[k, expert, target, :], w_sem.at[k, 2 * (block * EXP_G + expert)]))
                copies.append(pltpu.make_async_copy(wu_ref.at[expert, source, :], wub.at[k, expert, target, :], w_sem.at[k, 2 * (block * EXP_G + expert) + 1]))
        return copies

    def down_copies(k):
        copies = []
        for block in range(fold):
            source = pl.ds(pl.multiple_of(block * width + k * CHUNK, CHUNK), CHUNK)
            for expert in range(EXP_G):
                copies.append(pltpu.make_async_copy(
                    wd_ref.at[expert, :, source],
                    wdb.at[k, pl.ds(expert * hidden, hidden), pl.ds(block * CHUNK, CHUNK)],
                    d_sem.at[k, block * EXP_G + expert],
                ))
        return copies

    def own_z(k, step):
        return send(x_ref.at[k], xb.at[k, core, side, z], az_s.at[k, step], az_r.at[k, step], at(z_of(step), side, core))

    def side_hop(k, step):
        spot = xb.at[k, core, side, z_of(step)]
        source = x_ref.at[k] if step == 0 else spot
        return send(source, spot, ay_s.at[k, step], ay_r.at[k, step], side_dev)

    def core_hop(k, half, half_index):
        return send(xb.at[k, core, half], xb.at[k, core, half], ac_s.at[k, half_index], ac_r.at[k, half_index], core_dev)

    def own_local(k):
        return pltpu.make_async_copy(x_ref.at[k], xb.at[k, core, side, z], own_sem.at[k])

    def route_z(step):
        return send(r_ref, rb.at[core, side, z], az_s.at[chunks, step], az_r.at[chunks, step], at(z_of(step), side, core))

    def route_side():
        return send(rb.at[core, side], rb.at[core, side], ay_s.at[chunks, 0], ay_r.at[chunks, 0], side_dev)

    def route_core():
        return send(rb.at[core], rb.at[core], ac_s.at[chunks, 0], ac_r.at[chunks, 0], core_dev)

    def route_local():
        return pltpu.make_async_copy(r_ref, rb.at[core, side, z], own_sem.at[chunks])

    for k in range(2):
        for copy in up_copies(k):
            copy.start()
    for k in range(chunks):
        own_local(k).start()
    route_local().start()

    barrier = pltpu.get_barrier_semaphore()
    for step in range(1, zs):
        pl.semaphore_signal(barrier, inc=1, device_id=at(z_of(step), side, core), device_id_type=pl.DeviceIdType.MESH)
    pl.semaphore_signal(barrier, inc=1, device_id=side_dev, device_id_type=pl.DeviceIdType.MESH)
    pl.semaphore_signal(barrier, inc=1, device_id=core_dev, device_id_type=pl.DeviceIdType.MESH)
    pl.semaphore_wait(barrier, zs + 1)

    @pl.loop(0, chunks)
    def _(k):
        side_hop(k, 0).start()
        for step in range(1, zs):
            own_z(k, step).start()

        @pl.when(k == 0)
        def _():
            for step in range(1, zs):
                route_z(step).start()

    @pl.loop(2, chunks)
    def _(k):
        for copy in up_copies(k):
            copy.start()

    @pl.loop(0, chunks)
    def _(k):
        for copy in down_copies(k):
            copy.start()

    size = fold * band
    def order(index):
        first = floor_div(index, band)
        rest = index - first * band
        second = floor_div(rest, rows)
        return second * band + first * rows + (rest - second * rows)

    perm[...] = (order(iota_f32((size, 1), 0)) == iota_f32((size, size), 1)).astype(F32).astype(BF16)
    perm_back[...] = (iota_f32((size, size), 0) == order(iota_f32((1, size), 1))).astype(F32).astype(BF16)
    acc[...] = jnp.zeros_like(acc)

    @pl.loop(0, chunks + 2)
    def _(now):
        @pl.when(now < chunks)
        def _():
            k = now
            for step in range(1, zs):
                back = zs - step
                send(x_ref.at[k], xb.at[k, core, side, z_of(back)], az_s.at[k, step], az_r.at[k, step], at(z_of(back), side, core)).wait_recv()
                side_hop(k, back).start()
            own_local(k).wait()
            core_hop(k, side, 0).start()

            @pl.when(k == 0)
            def _():
                route_local().wait()
                for step in range(1, zs):
                    route_z(step).wait_recv()
                route_side().start()

        @pl.when((now >= 1) & (now < chunks + 1))
        def _():
            k = now - 1
            for step in range(zs):
                spot = xb.at[k, core, other_side, z_of(step)]
                send(spot, spot, ay_s.at[k, step], ay_r.at[k, step], side_dev).wait_recv()
            core_hop(k, other_side, 1).start()

            @pl.when(k == 0)
            def _():
                send(rb.at[core, other_side], rb.at[core, other_side], ay_s.at[chunks, 0], ay_r.at[chunks, 0], side_dev).wait_recv()
                route_core().start()

        @pl.when(now >= 2)
        def _():
            k = now - 2
            for half_index, half in ((0, side), (1, other_side)):
                spot = xb.at[k, other_core, half]
                send(spot, spot, ac_s.at[k, half_index], ac_r.at[k, half_index], core_dev).wait_recv()
            for copy in up_copies(k):
                copy.wait()
            folded = xb[k].reshape(groups, size, CHUNK)
            straight = []
            for group in range(groups):
                moved = jnp.dot(perm[...], folded[group], preferred_element_type=F32).astype(BF16)
                straight.append(jnp.concatenate([moved[block * band:(block + 1) * band] for block in range(fold)], axis=1))
            left = jnp.concatenate(straight, axis=0)
            for expert in range(EXP_G):
                acc[2 * expert] += jnp.dot(left, wgb[k, expert], preferred_element_type=F32)
                acc[2 * expert + 1] += jnp.dot(left, wub[k, expert], preferred_element_type=F32)

    route_core_spot = rb.at[other_core]
    send(route_core_spot, route_core_spot, ac_s.at[chunks, 0], ac_r.at[chunks, 0], core_dev).wait_recv()
    total = units * rows
    line = iota_f32((1, units * pad_rows), 1)
    unit_of = floor_div(line, pad_rows)
    row_of = line - unit_of * pad_rows
    wanted = jnp.where(row_of < rows, unit_of * rows + row_of, -1.0)
    pick = (iota_f32((total, units * pad_rows), 0) == wanted).astype(F32).astype(BF16)
    scales = jnp.dot(pick, rb[...].reshape(units * pad_rows, LANES), preferred_element_type=F32)
    lane = lax.broadcasted_iota(jnp.int32, (total, LANES), 1)
    first_expert = me // (wide // GROUPS) * EXP_G
    for expert in range(EXP_G):
        scale = jnp.sum(jnp.where(lane == first_expert + expert, scales, 0.0), axis=1, keepdims=True)
        gate = acc[2 * expert]
        value = gate / (1.0 + jnp.exp(-gate)) * acc[2 * expert + 1]
        hid[:, expert * hidden:(expert + 1) * hidden] = (value * scale).astype(BF16)

    def back_core(k):
        return send(packed.at[k, other_core], got_core.at[k], bc_s.at[k], bc_r.at[k], core_dev)

    def back_side(k):
        return send(sum_side.at[k, other_side], got_side.at[k], by_s.at[k], by_r.at[k], side_dev)

    def back_z(k, step):
        return send(sum_z.at[k, z_of(step)], got_z.at[k, step], bz_s.at[k, step], bz_r.at[k, step], at(z_of(step), side, core))

    @pl.loop(0, chunks + 3)
    def _(now):
        @pl.when(now < chunks)
        def _():
            k = now
            for copy in down_copies(k):
                copy.wait()
            down = jnp.dot(hid[...], wdb[k], preferred_element_type=F32).astype(BF16)
            sets = []
            for group in range(groups):
                lines = down[group * band:(group + 1) * band]
                stacked = jnp.concatenate([lines[:, block * CHUNK:(block + 1) * CHUNK] for block in range(fold)], axis=0)
                sets.append(jnp.dot(perm_back[...], stacked, preferred_element_type=F32).astype(BF16))
            packed[k] = jnp.concatenate(sets, axis=0).reshape(CORES, SIDES, zs, unit, CHUNK)
            back_core(k).start()

        @pl.when((now >= 1) & (now < chunks + 1))
        def _():
            k = now - 1
            back_core(k).wait_recv()
            sum_side[k] = (packed[k, core].astype(F32) + got_core[k].astype(F32)).astype(BF16)
            back_side(k).start()

        @pl.when((now >= 2) & (now < chunks + 2))
        def _():
            k = now - 2
            back_side(k).wait_recv()
            sum_z[k] = (sum_side[k, side].astype(F32) + got_side[k].astype(F32)).astype(BF16)
            for step in range(1, zs):
                back_z(k, step).start()

        @pl.when(now >= 3)
        def _():
            k = now - 3
            done = sum_z[k, z].astype(F32)
            for step in range(1, zs):
                back_z(k, step).wait_recv()
                done = done + got_z[k, step].astype(F32)
            out_buf[k] = done.astype(BF16)
            pltpu.make_async_copy(out_buf.at[k], out_ref.at[k], out_sem.at[k]).start()

    @pl.loop(0, chunks)
    def _(k):
        for step in range(1, zs):
            own_z(k, step).wait_send()
            back_z(k, step).wait_send()
        for step in range(zs):
            side_hop(k, step).wait_send()
        core_hop(k, side, 0).wait_send()
        core_hop(k, other_side, 1).wait_send()
        back_core(k).wait_send()
        back_side(k).wait_send()
        pltpu.make_async_copy(out_buf.at[k], out_ref.at[k], out_sem.at[k]).wait()

    for step in range(1, zs):
        route_z(step).wait_send()
    route_side().wait_send()
    route_core().wait_send()


def local(wide, interpret, tokens, expert_ids, gates, w_gate, w_up, w_down):
    rows, model = tokens.shape
    hidden = w_gate.shape[2]
    fold = 16 // math.gcd(16, rows)
    width = model // fold
    chunks = width // CHUNK
    zs = wide // (CORES * SIDES)
    pad_rows = -(-rows // 16) * 16
    unit = rows * fold
    size = fold * unit
    total = wide * rows

    x = tokens.reshape(rows, fold, chunks, CHUNK).transpose(2, 1, 0, 3).reshape(chunks, unit, CHUNK)
    lanes = jnp.arange(LANES, dtype=jnp.int32)
    picked = expert_ids[:, :, None] == lanes[None, None, :]
    route = jnp.sum(jnp.where(picked, gates[:, :, None], 0.0), axis=1).astype(BF16)
    route = jnp.pad(route, ((0, pad_rows - rows), (0, 0)))

    any_space = pl.BlockSpec(memory_space=pl.ANY)
    dma = pltpu.SemaphoreType.DMA
    out = pl.pallas_call(
        functools.partial(kernel, wide, rows, fold),
        out_shape=jax.ShapeDtypeStruct((chunks, unit, CHUNK), BF16),
        in_specs=[any_space] * 5,
        out_specs=any_space,
        scratch_shapes=[
            pltpu.VMEM((chunks, CORES, SIDES, zs, unit, CHUNK), BF16),
            pltpu.VMEM((CORES, SIDES, zs, pad_rows, LANES), BF16),
            pltpu.VMEM((chunks, EXP_G, fold * CHUNK, hidden), BF16),
            pltpu.VMEM((chunks, EXP_G, fold * CHUNK, hidden), BF16),
            pltpu.VMEM((chunks, EXP_G * hidden, fold * CHUNK), BF16),
            pltpu.VMEM((2 * EXP_G, total, hidden), F32),
            pltpu.VMEM((total, EXP_G * hidden), BF16),
            pltpu.VMEM((size, size), BF16),
            pltpu.VMEM((size, size), BF16),
            pltpu.VMEM((chunks, CORES, SIDES, zs, unit, CHUNK), BF16),
            pltpu.VMEM((chunks, SIDES, zs, unit, CHUNK), BF16),
            pltpu.VMEM((chunks, SIDES, zs, unit, CHUNK), BF16),
            pltpu.VMEM((chunks, zs, unit, CHUNK), BF16),
            pltpu.VMEM((chunks, zs, unit, CHUNK), BF16),
            pltpu.VMEM((chunks, zs, unit, CHUNK), BF16),
            pltpu.VMEM((chunks, unit, CHUNK), BF16),
            dma((chunks, 2 * EXP_G * fold)),
            dma((chunks, EXP_G * fold)),
            dma((chunks + 1,)),
            dma((chunks + 1, zs)), dma((chunks + 1, zs)),
            dma((chunks + 1, zs)), dma((chunks + 1, zs)),
            dma((chunks + 1, 2)), dma((chunks + 1, 2)),
            dma((chunks, zs)), dma((chunks, zs)),
            dma((chunks,)), dma((chunks,)),
            dma((chunks,)), dma((chunks,)),
            dma((chunks,)),
        ],
        compiler_params=pltpu.CompilerParams(collective_id=0, has_side_effects=True, vmem_limit_bytes=67043328),
        **interpret,
    )(x, route, w_gate, w_up, w_down)
    return out.reshape(chunks, fold, rows, CHUNK).transpose(2, 1, 0, 3).reshape(rows, model)


def solution(mesh, interpret=None):
    return jax.shard_map(
        functools.partial(local, mesh.shape["wide"], interpret or {}),
        mesh=mesh,
        in_specs=(
            P(("parts", "wide"), None),
            P(("parts", "wide"), None),
            P(("parts", "wide"), None),
            P(None, None, "wide"),
            P(None, None, "wide"),
            P(None, "wide", None),
        ),
        out_specs=P(("parts", "wide"), None),
        check_vma=False,
    )
```

time: 192 us -> 71.4 us (0.37)
  the two profiles are of different devices: /device:TPU:15 before, /device:TPU:0 now
where the time goes in v1:
time: 71.4 us; the launch traced here: 71.2 us
  Pallas kernels  65.1 us (91%)
  local copies, waits for them, and re-layouts  5.92 us (8%)
    pallas_call x1, Pallas kernels, local(): pl.pallas_call(functools.partial(kernel, wide, rows, fold), out_shape=jax...  65.1 us
    reshape x2, local copies, waits for them, and re-layouts, local(): tokens.reshape(rows, fold, chunks, CHUNK).transpose(2, 1, 0, 3)  1.88 us
    unnamed x2, local copies, waits for them, and re-layouts  1.54 us

profile of v1, /device:TPU:0, one launch (start us, length us, event | category | flops | bytes accessed | tf_op | source)
XLA Modules:
  0.0 71.2 jit_solution(2532414382686240601)
XLA Ops:
  0.0 0.8 %copy.18 = s32[12,8]{1,0:T(8,128)S(1)} copy(s32[12,8]{0,1:T(8,128)} %param.7) | data formatting | bytes 768 | tf_op args[1]
  0.8 0.8 %copy.19 = f32[12,8]{1,0:T(8,128)S(1)} copy(f32[12,8]{0,1:T(8,128)} %param.8) | data formatting | bytes 768 | tf_op args[2]
  1.5 0.1 select_reduce_fusion
  1.6 0.6 pad.4.r_ref
  2.3 1.2 %reshape.14 = bf16[12,4,7,256]{3,2,1,0:T(8,128)(2,1)S(1)} reshape(bf16[12,7168]{1,0:T(8,128)(2,1)} %param.6) | data formatting | bytes 344064 | tf_op jit(solution)/shard_map/reshape | solution.py:309
  3.5 0.7 copy.20.x_ref
  4.2 65.1 %shard_map.64 = bf16[7,48,256]{2,1,0:T(8,128)(2,1)} custom-call(bf16[7,48,256]{2,1,0:T(8,128)(2,1)} %copy.20.x_ref, bf16[16,128]{1,0:T(8,128)(2,1)} %pad.4.r_ref, bf16[2,7168,512]{2,1,0:T(8,128)(2,1)} %wg_ref.1, bf16[2,7168,512]{2,1,0:T(8,128)(2,1)} %wu_ref.1, bf16[2,512,7168]{2,1,0:T(8,128)(2,1)} %wd_ref.1), custom_call_target="tpu_custom_call" | custom-call | tf_op jit(solution)/shard_map/pallas_call | solution.py:317
  69.3 1.0 %copy.21 = bf16[7,48,256]{2,0,1:T(8,128)(2,1)S(1)} copy(bf16[7,48,256]{2,1,0:T(8,128)(2,1)} %shard_map.64) | data formatting | bytes 344064 | tf_op jit(solution)/shard_map/pallas_call | solution.py:317
  70.3 0.9 %reshape.17 = bf16[12,7168]{1,0:T(8,128)(2,1)} reshape(bf16[12,4,7,256]{3,2,1,0:T(8,128)(2,1)S(1)} %copy.22) | data formatting | bytes 344064 | tf_op jit(solution)/shard_map/reshape | solution.py:353
  (2 shorter events, 0.0 us)

commit v2 on v1

--- a/solution.py
+++ b/solution.py
@@ -14,6 +14,11 @@
 SIDES = 2
 CHUNK = 256
 LANES = 128
+LAG_SIDE = 3
+LAG_USE = 4
+LAG_SUM = 1
+LAG_Z = 4
+LAG_END = 7
 F32 = jnp.float32
 BF16 = jnp.bfloat16
 
@@ -28,9 +33,9 @@
 
 def kernel(
     wide, rows, fold,
-    x_ref, r_ref, wg_ref, wu_ref, wd_ref, out_ref,
-    xb, rb, wgb, wub, wdb, acc, hid, perm, perm_back, packed, got_core, sum_side, got_side, sum_z, got_z, out_buf,
-    w_sem, d_sem, own_sem, az_s, az_r, ay_s, ay_r, ac_s, ac_r, bz_s, bz_r, by_s, by_r, bc_s, bc_r, out_sem,
+    tok_ref, ids_ref, gate_ref, wg_ref, wu_ref, wd_ref, out_ref,
+    tok, x_ref, r_ref, xb, rb, wgb, wub, wdb, acc, hid, perm, perm_back, packed, got_core, sum_side, got_side, sum_z, got_z,
+    tok_sem, w_sem, d_sem, own_sem, az_s, az_r, ay_s, ay_r, ac_s, ac_r, bz_s, bz_r, by_s, by_r, bc_s, bc_r,
 ):
     zs = wide // (CORES * SIDES)
     chunks = x_ref.shape[0]
@@ -112,32 +117,40 @@
     def route_local():
         return pltpu.make_async_copy(r_ref, rb.at[core, side, z], own_sem.at[chunks])
 
-    for k in range(2):
-        for copy in up_copies(k):
-            copy.start()
-    for k in range(chunks):
-        own_local(k).start()
-    route_local().start()
+    token_copy = pltpu.make_async_copy(tok_ref, tok, tok_sem)
+    token_copy.start()
+    for copy in up_copies(0):
+        copy.start()
 
     barrier = pltpu.get_barrier_semaphore()
     for step in range(1, zs):
         pl.semaphore_signal(barrier, inc=1, device_id=at(z_of(step), side, core), device_id_type=pl.DeviceIdType.MESH)
     pl.semaphore_signal(barrier, inc=1, device_id=side_dev, device_id_type=pl.DeviceIdType.MESH)
     pl.semaphore_signal(barrier, inc=1, device_id=core_dev, device_id_type=pl.DeviceIdType.MESH)
-    pl.semaphore_wait(barrier, zs + 1)
-
-    @pl.loop(0, chunks)
-    def _(k):
+
+    lane = lax.broadcasted_iota(jnp.int32, (rows, LANES), 1)
+    route = jnp.zeros((rows, LANES), F32)
+    for slot in range(ids_ref.shape[1]):
+        route = route + jnp.where(ids_ref[:, slot:slot + 1] == lane, gate_ref[:, slot:slot + 1], 0.0)
+    spread = (iota_f32((pad_rows, rows), 0) == iota_f32((pad_rows, rows), 1)).astype(F32).astype(BF16)
+    r_ref[...] = jnp.dot(spread, route.astype(BF16), preferred_element_type=F32).astype(BF16)
+    route_local().start()
+    token_copy.wait()
+    place = iota_f32((unit, rows), 0) - iota_f32((unit, rows), 1)
+    into = [(place == block * rows).astype(F32).astype(BF16) for block in range(fold)]
+    for k in range(chunks):
+        parts = [jnp.dot(into[block], tok[:, block * width + k * CHUNK:block * width + (k + 1) * CHUNK], preferred_element_type=F32) for block in range(fold)]
+        x_ref[k] = sum(parts[1:], parts[0]).astype(BF16)
+        own_local(k).start()
+        if k == 0:
+            pl.semaphore_wait(barrier, zs + 1)
         side_hop(k, 0).start()
         for step in range(1, zs):
             own_z(k, step).start()
-
-        @pl.when(k == 0)
-        def _():
+        if k == 0:
             for step in range(1, zs):
                 route_z(step).start()
-
-    @pl.loop(2, chunks)
+    @pl.loop(1, chunks)
     def _(k):
         for copy in up_copies(k):
             copy.start()
@@ -158,7 +171,7 @@
     perm_back[...] = (iota_f32((size, size), 0) == order(iota_f32((1, size), 1))).astype(F32).astype(BF16)
     acc[...] = jnp.zeros_like(acc)
 
-    @pl.loop(0, chunks + 2)
+    @pl.loop(0, chunks + LAG_USE)
     def _(now):
         @pl.when(now < chunks)
         def _():
@@ -177,9 +190,9 @@
                     route_z(step).wait_recv()
                 route_side().start()
 
-        @pl.when((now >= 1) & (now < chunks + 1))
-        def _():
-            k = now - 1
+        @pl.when((now >= LAG_SIDE) & (now < chunks + LAG_SIDE))
+        def _():
+            k = now - LAG_SIDE
             for step in range(zs):
                 spot = xb.at[k, core, other_side, z_of(step)]
                 send(spot, spot, ay_s.at[k, step], ay_r.at[k, step], side_dev).wait_recv()
@@ -190,9 +203,9 @@
                 send(rb.at[core, other_side], rb.at[core, other_side], ay_s.at[chunks, 0], ay_r.at[chunks, 0], side_dev).wait_recv()
                 route_core().start()
 
-        @pl.when(now >= 2)
-        def _():
-            k = now - 2
+        @pl.when(now >= LAG_USE)
+        def _():
+            k = now - LAG_USE
             for half_index, half in ((0, side), (1, other_side)):
                 spot = xb.at[k, other_core, half]
                 send(spot, spot, ac_s.at[k, half_index], ac_r.at[k, half_index], core_dev).wait_recv()
@@ -234,7 +247,7 @@
     def back_z(k, step):
         return send(sum_z.at[k, z_of(step)], got_z.at[k, step], bz_s.at[k, step], bz_r.at[k, step], at(z_of(step), side, core))
 
-    @pl.loop(0, chunks + 3)
+    @pl.loop(0, chunks + LAG_END)
     def _(now):
         @pl.when(now < chunks)
         def _():
@@ -250,30 +263,34 @@
             packed[k] = jnp.concatenate(sets, axis=0).reshape(CORES, SIDES, zs, unit, CHUNK)
             back_core(k).start()
 
-        @pl.when((now >= 1) & (now < chunks + 1))
-        def _():
-            k = now - 1
+        @pl.when((now >= LAG_SUM) & (now < chunks + LAG_SUM))
+        def _():
+            k = now - LAG_SUM
             back_core(k).wait_recv()
             sum_side[k] = (packed[k, core].astype(F32) + got_core[k].astype(F32)).astype(BF16)
             back_side(k).start()
 
-        @pl.when((now >= 2) & (now < chunks + 2))
-        def _():
-            k = now - 2
+        @pl.when((now >= LAG_Z) & (now < chunks + LAG_Z))
+        def _():
+            k = now - LAG_Z
             back_side(k).wait_recv()
             sum_z[k] = (sum_side[k, side].astype(F32) + got_side[k].astype(F32)).astype(BF16)
             for step in range(1, zs):
                 back_z(k, step).start()
 
-        @pl.when(now >= 3)
-        def _():
-            k = now - 3
+        @pl.when(now >= LAG_END)
+        def _():
+            k = now - LAG_END
             done = sum_z[k, z].astype(F32)
             for step in range(1, zs):
                 back_z(k, step).wait_recv()
                 done = done + got_z[k, step].astype(F32)
-            out_buf[k] = done.astype(BF16)
-            pltpu.make_async_copy(out_buf.at[k], out_ref.at[k], out_sem.at[k]).start()
+            final = done.astype(BF16)
+            away = iota_f32((rows, unit), 1) - iota_f32((rows, unit), 0)
+            for block in range(fold):
+                out_of = (away == block * rows).astype(F32).astype(BF16)
+                spot = pl.ds(pl.multiple_of(block * width + k * CHUNK, CHUNK), CHUNK)
+                out_ref[:, spot] = jnp.dot(out_of, final, preferred_element_type=F32).astype(BF16)
 
     @pl.loop(0, chunks)
     def _(k):
@@ -286,7 +303,6 @@
         core_hop(k, other_side, 1).wait_send()
         back_core(k).wait_send()
         back_side(k).wait_send()
-        pltpu.make_async_copy(out_buf.at[k], out_ref.at[k], out_sem.at[k]).wait()
 
     for step in range(1, zs):
         route_z(step).wait_send()
@@ -306,20 +322,17 @@
     size = fold * unit
     total = wide * rows
 
-    x = tokens.reshape(rows, fold, chunks, CHUNK).transpose(2, 1, 0, 3).reshape(chunks, unit, CHUNK)
-    lanes = jnp.arange(LANES, dtype=jnp.int32)
-    picked = expert_ids[:, :, None] == lanes[None, None, :]
-    route = jnp.sum(jnp.where(picked, gates[:, :, None], 0.0), axis=1).astype(BF16)
-    route = jnp.pad(route, ((0, pad_rows - rows), (0, 0)))
-
     any_space = pl.BlockSpec(memory_space=pl.ANY)
     dma = pltpu.SemaphoreType.DMA
     out = pl.pallas_call(
         functools.partial(kernel, wide, rows, fold),
-        out_shape=jax.ShapeDtypeStruct((chunks, unit, CHUNK), BF16),
-        in_specs=[any_space] * 5,
-        out_specs=any_space,
+        out_shape=jax.ShapeDtypeStruct((rows, model), BF16),
+        in_specs=[any_space] + [pl.BlockSpec(memory_space=pltpu.VMEM)] * 2 + [any_space] * 3,
+        out_specs=pl.BlockSpec(memory_space=pltpu.VMEM),
         scratch_shapes=[
+            pltpu.VMEM((rows, model), BF16),
+            pltpu.VMEM((chunks, unit, CHUNK), BF16),
+            pltpu.VMEM((pad_rows, LANES), BF16),
             pltpu.VMEM((chunks, CORES, SIDES, zs, unit, CHUNK), BF16),
             pltpu.VMEM((CORES, SIDES, zs, pad_rows, LANES), BF16),
             pltpu.VMEM((chunks, EXP_G, fold * CHUNK, hidden), BF16),
@@ -335,7 +348,7 @@
             pltpu.VMEM((chunks, zs, unit, CHUNK), BF16),
             pltpu.VMEM((chunks, zs, unit, CHUNK), BF16),
             pltpu.VMEM((chunks, zs, unit, CHUNK), BF16),
-            pltpu.VMEM((chunks, unit, CHUNK), BF16),
+            dma(()),
             dma((chunks, 2 * EXP_G * fold)),
             dma((chunks, EXP_G * fold)),
             dma((chunks + 1,)),
@@ -345,12 +358,11 @@
             dma((chunks, zs)), dma((chunks, zs)),
             dma((chunks,)), dma((chunks,)),
             dma((chunks,)), dma((chunks,)),
-            dma((chunks,)),
         ],
         compiler_params=pltpu.CompilerParams(collective_id=0, has_side_effects=True, vmem_limit_bytes=67043328),
         **interpret,
-    )(x, route, w_gate, w_up, w_down)
-    return out.reshape(chunks, fold, rows, CHUNK).transpose(2, 1, 0, 3).reshape(rows, model)
+    )(tokens, expert_ids, gates, w_gate, w_up, w_down)
+    return out
 
 
 def solution(mesh, interpret=None):

time: 71.4 us -> 63.3 us (0.89)
  Pallas kernels: 65.1 us -> 58.6 us
  local copies, waits for them, and re-layouts: 5.92 us -> 4.36 us
    pallas_call x1, Pallas kernels: 65.1 us -> 58.6 us  [local(): pl.pallas_call(functools.partial(kernel, wide, rows, fold), out_shape=jax...]
    unnamed x2 -> x3, local copies, waits for them, and re-layouts: 1.54 us -> 4.36 us
    reshape x3 -> x0, local copies, waits for them, and re-layouts: 2.77 us -> none  [the longest x2 1.88 us: local(): tokens.reshape(rows, fold, chunks, CHUNK).transpose(2, 1, 0, 3)]
    pallas_call x1 -> x0, local copies, waits for them, and re-layouts: 0.98 us -> none  [local(): pl.pallas_call(functools.partial(kernel, wide, rows, fold), out_shape=jax...]
where the time goes in v2:
time: 63.3 us; the launch traced here: 63 us
  Pallas kernels  58.6 us (93%)
  local copies, waits for them, and re-layouts  4.36 us (7%)
    pallas_call x1, Pallas kernels, local(): pl.pallas_call(functools.partial(kernel, wide, rows, fold), out_shape=jax...  58.6 us
    unnamed x3, local copies, waits for them, and re-layouts  4.36 us

profile of v2, /device:TPU:0, one launch (start us, length us, event | category | flops | bytes accessed | tf_op | source)
XLA Modules:
  0.0 63.0 jit_solution(383077246284801192)
XLA Ops:
  0.0 1.4 %copy.7.ids_ref = s32[12,8]{1,0:T(8,128)} copy(s32[12,8]{0,1:T(8,128)} %param.7) | data formatting | bytes 768 | tf_op args[1]
  1.4 1.4 %copy.8.gate_ref = f32[12,8]{1,0:T(8,128)} copy(f32[12,8]{0,1:T(8,128)} %param.8) | data formatting | bytes 768 | tf_op args[2]
  2.7 58.6 %shard_map.64 = bf16[12,7168]{1,0:T(8,128)(2,1)} custom-call(bf16[12,7168]{1,0:T(8,128)(2,1)} %tok_ref.1, s32[12,8]{1,0:T(8,128)} %copy.7.ids_ref, f32[12,8]{1,0:T(8,128)} %copy.8.gate_ref, bf16[2,7168,512]{2,1,0:T(8,128)(2,1)} %wg_ref.1, bf16[2,7168,512]{2,1,0:T(8,128)(2,1)} %wu_ref.1, bf16[2,512,7168]{2,1,0:T(8,128)(2,1)} %wd_ref.1), custom_call_target="tpu_custom_call" | custom-call | tf_op jit(solution)/shard_map/pallas_call | solution.py:327
  61.4 1.6 %copy.10 = bf16[12,7168]{1,0:T(8,128)(2,1)} copy(bf16[12,7168]{1,0:T(8,128)(2,1)} %shard_map.64) | data formatting | bytes 344064

commit v3 on v2

--- a/solution.py
+++ b/solution.py
@@ -74,9 +74,8 @@
         for block in range(fold):
             source = pl.ds(pl.multiple_of(block * width + k * CHUNK, CHUNK), CHUNK)
             target = pl.ds(block * CHUNK, CHUNK)
-            for expert in range(EXP_G):
-                copies.append(pltpu.make_async_copy(wg_ref.at[expert, source, :], wgb.at[k, expert, target, :], w_sem.at[k, 2 * (block * EXP_G + expert)]))
-                copies.append(pltpu.make_async_copy(wu_ref.at[expert, source, :], wub.at[k, expert, target, :], w_sem.at[k, 2 * (block * EXP_G + expert) + 1]))
+            copies.append(pltpu.make_async_copy(wg_ref.at[:, source, :], wgb.at[k, :, target, :], w_sem.at[k, 2 * block]))
+            copies.append(pltpu.make_async_copy(wu_ref.at[:, source, :], wub.at[k, :, target, :], w_sem.at[k, 2 * block + 1]))
         return copies
 
     def down_copies(k):
@@ -150,16 +149,6 @@
         if k == 0:
             for step in range(1, zs):
                 route_z(step).start()
-    @pl.loop(1, chunks)
-    def _(k):
-        for copy in up_copies(k):
-            copy.start()
-
-    @pl.loop(0, chunks)
-    def _(k):
-        for copy in down_copies(k):
-            copy.start()
-
     size = fold * band
     def order(index):
         first = floor_div(index, band)
@@ -182,6 +171,14 @@
                 side_hop(k, back).start()
             own_local(k).wait()
             core_hop(k, side, 0).start()
+
+            @pl.when(k + 1 < chunks)
+            def _():
+                for copy in up_copies(k + 1):
+                    copy.start()
+
+            for copy in down_copies(k):
+                copy.start()
 
             @pl.when(k == 0)
             def _():
@@ -349,7 +346,7 @@
             pltpu.VMEM((chunks, zs, unit, CHUNK), BF16),
             pltpu.VMEM((chunks, zs, unit, CHUNK), BF16),
             dma(()),
-            dma((chunks, 2 * EXP_G * fold)),
+            dma((chunks, 2 * fold)),
             dma((chunks, EXP_G * fold)),
             dma((chunks + 1,)),
             dma((chunks + 1, zs)), dma((chunks + 1, zs)),

time: 63.3 us -> 62.7 us (level)
    pallas_call x1, Pallas kernels: 58.6 us -> 58 us  [local(): pl.pallas_call(functools.partial(kernel, wide, rows, fold), out_shape=jax...]
where the time goes in v3:
time: 62.7 us; the launch traced here: 62.4 us
  Pallas kernels  58 us (93%)
  local copies, waits for them, and re-layouts  4.36 us (7%)
    pallas_call x1, Pallas kernels, local(): pl.pallas_call(functools.partial(kernel, wide, rows, fold), out_shape=jax...  58 us
    unnamed x3, local copies, waits for them, and re-layouts  4.36 us

profile of v3, /device:TPU:0, one launch (start us, length us, event | category | flops | bytes accessed | tf_op | source)
XLA Modules:
  0.0 62.4 jit_solution(14550612581904163750)
XLA Ops:
  0.0 1.4 %copy.7.ids_ref = s32[12,8]{1,0:T(8,128)} copy(s32[12,8]{0,1:T(8,128)} %param.7) | data formatting | bytes 768 | tf_op args[1]
  1.4 1.4 %copy.8.gate_ref = f32[12,8]{1,0:T(8,128)} copy(f32[12,8]{0,1:T(8,128)} %param.8) | data formatting | bytes 768 | tf_op args[2]
  2.7 58.0 %shard_map.64 = bf16[12,7168]{1,0:T(8,128)(2,1)} custom-call(bf16[12,7168]{1,0:T(8,128)(2,1)} %tok_ref.1, s32[12,8]{1,0:T(8,128)} %copy.7.ids_ref, f32[12,8]{1,0:T(8,128)} %copy.8.gate_ref, bf16[2,7168,512]{2,1,0:T(8,128)(2,1)} %wg_ref.1, bf16[2,7168,512]{2,1,0:T(8,128)(2,1)} %wu_ref.1, bf16[2,512,7168]{2,1,0:T(8,128)(2,1)} %wd_ref.1), custom_call_target="tpu_custom_call" | custom-call | tf_op jit(solution)/shard_map/pallas_call | solution.py:324
  60.7 1.6 %copy.10 = bf16[12,7168]{1,0:T(8,128)(2,1)} copy(bf16[12,7168]{1,0:T(8,128)(2,1)} %shard_map.64) | data formatting | bytes 344064
